TPU v7x, 32 devices: a whole 2x2x4 slice. The times are simulated.
32 devices in a mesh: groups: 2 (over x), seq: 16 (over z, y, core).
Axes of the slice: x: 2, y: 2, z: 4, core: 2. Of those that a mesh axis runs over, the one named last changes fastest.
Arguments:
- features: bfloat16 [2, 2048, 640], P('groups', 'seq'), parts along dimension 0, may hold values from -18 to 18
- gain_first: float32 [640], replicated, may hold values from 0.1 to 1.9
- weight_first: bfloat16 [640, 3840], replicated, may hold values from -0.109375 to 0.109375
- gain_second: float32 [768], replicated, may hold values from 0.1 to 1.9
- weight_second: bfloat16 [768, 3840], replicated, may hold values from -0.09375 to 0.09375
- upstream: bfloat16 [2, 512, 768], P('groups', 'seq'), parts along dimension 0, may hold values from -4 to 4
Outputs:
- encoded: bfloat16 [2, 512, 768], P('groups', 'seq'), parts along dimension 0
- input_grad: bfloat16 [2, 2048, 640], P('groups', 'seq'), parts along dimension 0
- weight_first_grad: float32 [1280, 3840], P(('groups', 'seq')), parts along dimension 0
- weight_second_grad: float32 [1536, 3840], P(('groups', 'seq')), parts along dimension 0
- gain_first_grad: float32 [1280], P('groups'), parts along dimension 0
- gain_second_grad: float32 [1536], P('groups'), parts along dimension 0
There are 2 independent parts, one for each index of `groups`. A program takes and returns all parts, laid end to end along the dimension named above; an argument that names none is the same for every part. Nothing has to cross between parts.
All inputs are finite; a program needn't handle non-finite values.
Results may differ from a plain program's by a relative error of at most 0.0053.
Values may be sent and summed in bfloat16 or wider, within the bound.
A program may use at most 128 MiB of HBM per device.

v0:
```python
import jax
import jax.numpy as jnp
from jax import lax
from jax.sharding import PartitionSpec as P

KERNEL = 5


def extended(shard, sides, width):
    for axis, dim in sides:
        devices, length = (lax.axis_size(axis), shard.shape[dim])
        up = [(i, (i + 1) % devices) for i in range(devices - 1)]
        down = [(j, i) for i, j in up]
        last = lax.slice_in_dim(shard, length - width, length, axis=dim)
        leading = lax.slice_in_dim(shard, 0, width, axis=dim)
        before = lax.ppermute(last, axis, up)
        after = lax.ppermute(leading, axis, down)
        shard = jnp.concatenate([before, shard, after], axis=dim)
    return shard


def norm_gelu(values, gain):
    floats = values.astype(jnp.float32)
    inverse = lax.rsqrt(jnp.mean(floats * floats, axis=-1, keepdims=True) + 1e-06)
    normed = floats * inverse * gain
    return (floats, normed, inverse, jax.nn.gelu(normed).astype(jnp.bfloat16))


def with_rims(values, width):
    return extended(values, (("seq", 1),), width)


def forward_section(wide, gain, weight):
    chan_in = wide.shape[-1]
    chan_out = weight.shape[1] // KERNEL
    half_kernel = KERNEL // 2
    floats, normed, inverse, hidden = norm_gelu(wide, gain)
    projected = jnp.dot(hidden, weight, preferred_element_type=jnp.float32)
    interior = wide.shape[1] - 2 * half_kernel
    conv_sum = projected[:, 0:interior, 0:chan_out]
    for k in range(1, KERNEL):
        conv_sum = conv_sum + projected[:, k : k + interior, k * chan_out : (k + 1) * chan_out]
    summed = conv_sum + jnp.pad(
        floats[:, half_kernel : half_kernel + interior], ((0, 0), (0, 0), (0, chan_out - chan_in))
    )
    pooled = ((summed[:, 0::2] + summed[:, 1::2]) * 0.5).astype(jnp.bfloat16)
    return (pooled, (floats, normed, inverse, hidden))


def backward_section(upper, rim_up, saved, rim_saved, gain, weight):
    floats, normed, inverse, hidden = saved
    chan_in = floats.shape[-1]
    half_kernel = KERNEL // 2
    spread = jnp.repeat(upper, 2, axis=1) * 0.5
    interior = spread.shape[1] - 2 * half_kernel
    stacked = jnp.concatenate(
        [spread[:, 2 * half_kernel - k : 2 * half_kernel - k + interior] for k in range(KERNEL)],
        axis=-1,
    )
    back_acts = lax.dot_general(
        stacked, weight, (((2,), (1,)), ((), ())), preferred_element_type=jnp.float32
    )
    rim_out = 2 * rim_up - half_kernel
    offset = rim_saved - rim_out
    floats_here = floats[:, offset : offset + interior]
    normed_here = normed[:, offset : offset + interior]
    inverse_here = inverse[:, offset : offset + interior]
    _, pullback = jax.vjp(jax.nn.gelu, normed_here)
    grad_norm = pullback(back_acts)[0]
    scaled = grad_norm * gain
    own_terms = grad_norm * floats_here * inverse_here
    gain_part = jnp.sum(own_terms, axis=(0, 1))
    grad_x = inverse_here * scaled - floats_here * inverse_here**3 * jnp.mean(
        scaled * floats_here, axis=-1, keepdims=True
    )
    grad_x = grad_x + spread[:, half_kernel : half_kernel + interior, :chan_in].astype(jnp.float32)
    return (grad_x.astype(jnp.bfloat16), rim_out, gain_part)


def weight_grads(hidden_ext, rim, own_len, cotangent):
    half_kernel = KERNEL // 2
    hidden_own = hidden_ext[:, rim : rim + own_len]
    columns = lax.all_to_all(hidden_own, "seq", split_axis=2, concat_axis=1, tiled=True)
    whole = lax.all_gather(cotangent, "seq", axis=1, tiled=True)
    spread = jnp.repeat(whole, 2, axis=1) * 0.5
    length = columns.shape[1]
    padded = jnp.pad(columns, ((0, 0), (half_kernel, half_kernel), (0, 0)))
    blocks = []
    for k in range(KERNEL):
        blocks.append(
            jnp.einsum(
                "blc,blo->co", padded[:, k : k + length], spread, preferred_element_type=jnp.float32
            )
        )
    return jnp.concatenate(blocks, axis=1)


def shards(features, gain_first, weight_first, gain_second, weight_second, upstream):
    own_first = features.shape[1]
    own_second = own_first // 2
    rim_first = 2
    rim_upper = 1
    wide_first = with_rims(features, rim_first)
    middle, saved_first = forward_section(wide_first, gain_first, weight_first)
    wide_second = with_rims(middle, 2)
    encoded, saved_second = forward_section(wide_second, gain_second, weight_second)
    upper_ext = with_rims(upstream, rim_upper)
    middle_grad, rim_mid, gain_second_part = backward_section(
        upper_ext, rim_upper, saved_second, 2, gain_second, weight_second
    )
    lower_ext = with_rims(middle_grad, 1)
    input_grad, rim_low, gain_first_part = backward_section(
        lower_ext, 1, saved_first, rim_first, gain_first, weight_first
    )
    weight_second_grad = weight_grads(saved_second[3], 2, own_second, upstream)
    weight_first_grad = weight_grads(saved_first[3], rim_first, own_first, middle_grad)
    gain_totals = lax.psum((gain_first_part, gain_second_part), "seq")
    return (
        encoded,
        input_grad,
        weight_first_grad,
        weight_second_grad,
        gain_totals[0],
        gain_totals[1],
    )


def solution(mesh):
    placed = (P("groups", "seq", None), P(), P(), P(), P(), P("groups", "seq", None))
    return jax.shard_map(
        shards,
        mesh=mesh,
        in_specs=placed,
        out_specs=(
            P("groups", "seq", None),
            P("groups", "seq", None),
            P(("groups", "seq"), None),
            P(("groups", "seq"), None),
            P("groups"),
            P("groups"),
        ),
        check_vma=False,
    )
```

profile of v0, /device:TPU:0, one launch (start us, length us, event | category | flops | bytes accessed | tf_op | source)
XLA Modules:
  0.0 158.3 jit_solution(17065263145567495569)
XLA Ops:
  7.9 2.3 %collective-permute-start = (bf16[1,2,640]{2,1,0:T(2,128)(2,1)S(1)}, bf16[1,2,640]{2,1,0:T(2,128)(2,1)S(1)}, u32[]{:S(2)}, u32[]{:S(2)}) collective-permute-start(bf16[1,2,640]{2,1,0:T(2,128)(2,1)S(1)} %get-tuple-element.16), channel_id=1, source_target_pairs={{0,1},{1,2},{2,3},{3,4},{4,5},{5,6},{6,7},{7,8},{8,9},{9,10},{10,1... | collective-permute-start | bytes 7688 | tf_op jit(solution)/shard_map/ppermute | solution.py:16
  10.3 1.3 collective-permute-start.1
  12.3 5.2 %collective-permute-start.4 = (bf16[1,1,768]{2,1,0:T(2,128)(2,1)S(1)}, bf16[1,1,768]{2,1,0:T(2,128)(2,1)S(1)}, u32[]{:S(2)}, u32[]{:S(2)}) collective-permute-start(bf16[1,1,768]{2,1,0:T(2,128)(2,1)S(1)} %get-tuple-element.24), channel_id=1, source_target_pairs={{0,1},{1,2},{2,3},{3,4},{4,5},{5,6},{6,7},{7,8},{8,9},{9,10},{10,1... | collective-permute-start | bytes 4616 | tf_op jit(solution)/shard_map/ppermute | solution.py:16
  17.5 1.3 collective-permute-start.5
  18.8 26.5 %all_gather.7 = bf16[1,512,768]{2,1,0:T(8,128)(2,1)S(1)} all-gather(bf16[1,32,768]{2,1,0:T(8,128)(2,1)} %param.11), channel_id=1, replica_groups=mesh['groups'=2,'seq'=16] {'seq'}, dimensions={1}, use_global_device_ids=true | all-gather | bytes 835584 | tf_op jit(solution)/shard_map/all_gather | solution.py:84
  48.1 3.6 %convolution_bitcast_fusion = f32[1,132,3840]{2,1,0:T(8,128)S(1)} fusion(bf16[640,3840]{1,0:T(8,128)(2,1)} %param.8, bf16[2,640]{1,0:T(2,128)(2,1)S(1)} %bitcast.134, bf16[128,640]{1,0:T(8,128)(2,1)S(1)} %bitcast.121, bf16[2,640]{1,0:T(2,128)(2,1)S(1)} %bitcast.133, f32[640]{0:T(1024)S(1)} %copy-done.4, f32[132]{0:T(256)S(1)} %add_rsqrt_fusion), kind=kOutput, calls=%fused_computation | convolution fusion | flops 650242560 | bytes 7114768 | tf_op jit(solution)/shard_map/dot_general | solution.py:38
  52.2 2.3 %collective-permute-start.2 = (bf16[1,2,768]{2,1,0:T(2,128)(2,1)S(1)}, bf16[1,2,768]{2,1,0:T(2,128)(2,1)S(1)}, u32[]{:S(2)}, u32[]{:S(2)}) collective-permute-start(bf16[1,2,768]{2,1,0:T(2,128)(2,1)S(1)} %get-tuple-element.22), channel_id=1, source_target_pairs={{0,1},{1,2},{2,3},{3,4},{4,5},{5,6},{6,7},{7,8},{8,9},{9,10},{10,1... | collective-permute-start | bytes 9224 | tf_op jit(solution)/shard_map/ppermute | solution.py:16
  54.4 1.3 collective-permute-start.3
  56.8 1.6 %reduce.4 = bf16[640,128]{1,0:T(8,128)(2,1)S(1)} reduce(bf16[640,1,128]{2,1,0:T(2,128)(2,1)S(1)} %bitcast.127, bf16[]{:T(256)} %broadcast.445), dimensions={1}, to_apply=%bitcast.93.reduce_sub_computation | reduce | bytes 327682
  59.6 4.9 %multiply_reduce_fusion.4 = (f32[768]{0:T(1024)S(1)}, f32[64]{0:T(128)S(1)}, f32[1,64,768]{2,1,0:T(8,128)S(1)}) fusion(f32[1,68,768]{2,1,0:T(8,128)S(1)} %maximum_convert_fusion.1, f32[64]{0:T(128)S(1)} %get-tuple-element.29, f32[768]{0:T(1024)S(1)} %copy-done.3, f32[1,68,768]{2,1,0:T(8,128)S(1)} %get-tuple-element.19, bf16[768,3840]{1,0:T(8,128)(2,1)} %param.10, ...), kind=kOutput, calls=%fused_computation.92 | convolution fusion | flops 378715328 | bytes 6986240 | tf_op jit(solution)/shard_map/dot_general | solution.py:60
  64.5 3.9 %convolution_bitcast_fusion.1 = f32[1,68,3840]{2,1,0:T(8,128)S(1)} fusion(bf16[768,3840]{1,0:T(8,128)(2,1)} %param.10, bf16[2,768]{1,0:T(2,128)(2,1)S(1)} %bitcast.132, bf16[64,768]{1,0:T(8,128)(2,1)S(1)} %bitcast.122, bf16[2,768]{1,0:T(2,128)(2,1)S(1)} %bitcast.131, f32[768]{0:T(1024)S(1)} %copy-done.3, f32[68]{0:T(128)S(1)} %get-tuple-element.31), kind=kOutput, calls=%fused_computation.1 | convolution fusion | flops 401968128 | bytes 7050512 | tf_op jit(solution)/shard_map/dot_general | solution.py:38
  68.4 0.8 add_convert_fusion.1
  70.6 1.9 %reduce.5 = bf16[768,64]{1,0:T(8,128)(2,1)S(1)} reduce(bf16[768,1,64]{2,1,0:T(2,128)(2,1)S(1)} %bitcast.123, bf16[]{:T(256)} %broadcast.445), dimensions={1}, to_apply=%bitcast.95.reduce_sub_computation | reduce | bytes 196610
  73.3 3.6 %all-to-all-start.1 = ((bf16[16,2,1536]{2,1,0:T(2,128)(2,1)}), bf16[16,2,1536]{2,1,0:T(2,128)(2,1)S(1)}, u32[]{:S(2)}, u32[]{:S(2)}) async-start(bf16[16,2,1536]{2,1,0:T(2,128)(2,1)} %reshape.766), calls=%async_computation.1 | async-start | bytes 196608 | tf_op jit(solution)/shard_map/all_to_all | solution.py:83
  76.9 2.8 %collective-permute-start.6 = (bf16[1,1,768]{2,1,0:T(2,128)(2,1)S(1)}, bf16[1,1,768]{2,1,0:T(2,128)(2,1)S(1)}, u32[]{:S(2)}, u32[]{:S(2)}) collective-permute-start(bf16[1,1,768]{2,1,0:T(2,128)(2,1)S(1)} %get-tuple-element.20), channel_id=1, source_target_pairs={{0,1},{1,2},{2,3},{3,4},{4,5},{5,6},{6,7},{7,8},{8,9},{9,10},{10,1... | collective-permute-start | bytes 4616 | tf_op jit(solution)/shard_map/ppermute | solution.py:16
  79.7 1.3 collective-permute-start.7
  81.7 1.9 %collective-permute-done.7 = bf16[1,1,768]{2,1,0:T(2,128)(2,1)S(1)} collective-permute-done((bf16[1,1,768]{2,1,0:T(2,128)(2,1)S(1)}, bf16[1,1,768]{2,1,0:T(2,128)(2,1)S(1)}, u32[]{:S(2)}, u32[]{:S(2)}) %collective-permute-start.7) | collective-permute-done | bytes 1568 | tf_op jit(solution)/shard_map/ppermute | solution.py:17
  83.5 0.9 fusion.82
  84.9 4.2 %multiply_reduce_fusion.1 = (f32[640]{0:T(1024)S(1)}, f32[128]{0:T(128)S(1)}, f32[1,128,640]{2,1,0:T(8,128)S(1)}) fusion(f32[128]{0:T(128)S(1)} %get-tuple-element.27, f32[1,132,640]{2,1,0:T(8,128)S(1)} %maximum_convert_fusion, f32[640]{0:T(1024)S(1)} %copy-done.4, f32[1,132,640]{2,1,0:T(8,128)S(1)} %get-tuple-element.15, bf16[640,3840]{1,0:T(8,128)(2,1)} %param.8, ...), kind=kOutput, calls=%fused_computation.53 | convolution fusion | flops 631192832 | bytes 6887424 | tf_op jit(solution)/shard_map/dot_general | solution.py:60
  89.2 33.6 %all-reduce.3 = (f32[640]{0:T(1024)}, f32[768]{0:T(1024)}) all-reduce(f32[640]{0:T(1024)S(1)} %get-tuple-element.6, f32[768]{0:T(1024)S(1)} %get-tuple-element.8), channel_id=1, replica_groups=mesh['groups'=2,'seq'=16] {'seq'}, use_global_device_ids=true, to_apply=%region_5.6 | all-reduce | flops 1408 | bytes 11264 | tf_op jit(solution)/shard_map/psum | solution.py:117
  122.7 0.9 add_convert_fusion
  123.6 3.7 %all-to-all-start = ((bf16[16,2,2560]{2,1,0:T(2,128)(2,1)}), bf16[16,2,2560]{2,1,0:T(2,128)(2,1)S(1)}, u32[]{:S(2)}, u32[]{:S(2)}) async-start(bf16[16,2,2560]{2,1,0:T(2,128)(2,1)} %reshape.764), calls=%async_computation | async-start | bytes 327680 | tf_op jit(solution)/shard_map/all_to_all | solution.py:83
  128.8 1.1 convolution_dynamic-update-slice_fusion.4
  129.9 1.1 convolution_dynamic-update-slice_fusion.3
  131.0 1.0 convolution_dynamic-update-slice_fusion.2
  132.0 1.1 convolution_dynamic-update-slice_fusion.1
  133.1 1.1 convolution_dynamic-update-slice_fusion
  134.2 1.5 all-to-all-done
  136.0 1.5 multiply_bitcast_fusion
  137.5 3.3 %broadcast_in_dim.26 = bf16[1024,2,768]{2,1,0:T(2,128)(2,1)} broadcast(bf16[1024,768]{1,0:T(8,128)(2,1)S(1)} %multiply_bitcast_fusion), dimensions={0,2} | broadcast | bytes 4718592 | tf_op jit(solution)/shard_map/broadcast_in_dim | solution.py:85
  140.8 6.4 %broadcast_in_dim.27 = bf16[2048,768]{1,0:T(8,128)(2,1)S(1)} reshape(bf16[1024,2,768]{2,1,0:T(2,128)(2,1)} %broadcast_in_dim.26) | data formatting | bytes 6291456 | tf_op jit(solution)/shard_map/broadcast_in_dim | solution.py:85
  150.6 0.8 copy-done.5
  (86 shorter events, 15.0 us)
Async XLA Ops:
  7.2 128.8 %all-gather.2.cloned.1.call-start = ((), (), s32[]{:S(2)}) async-start(), calls=%async_computation.2 | async-start | bytes 1671168 | tf_op jit(solution)/shard_map/all_gather | solution.py:84
  7.9 39.3 %collective-permute-start = (bf16[1,2,640]{2,1,0:T(2,128)(2,1)S(1)}, bf16[1,2,640]{2,1,0:T(2,128)(2,1)S(1)}, u32[]{:S(2)}, u32[]{:S(2)}) collective-permute-start(bf16[1,2,640]{2,1,0:T(2,128)(2,1)S(1)} %get-tuple-element.16), channel_id=1, source_target_pairs={{0,1},{1,2},{2,3},{3,4},{4,5},{5,6},{6,7},{7,8},{8,9},{9,10},{10,1... | collective-permute-start | bytes 7688 | tf_op jit(solution)/shard_map/ppermute | solution.py:16
  10.3 36.9 %collective-permute-start.1 = (bf16[1,2,640]{2,1,0:T(2,128)(2,1)S(1)}, bf16[1,2,640]{2,1,0:T(2,128)(2,1)S(1)}, u32[]{:S(2)}, u32[]{:S(2)}) collective-permute-start(bf16[1,2,640]{2,1,0:T(2,128)(2,1)S(1)} %get-tuple-element.17), channel_id=1, source_target_pairs={{1,0},{2,1},{3,2},{4,3},{5,4},{6,5},{7,6},{8,7},{9,8},{10,9},{11,1... | collective-permute-start | bytes 7688 | tf_op jit(solution)/shard_map/ppermute | solution.py:17
  12.3 34.5 %collective-permute-start.4 = (bf16[1,1,768]{2,1,0:T(2,128)(2,1)S(1)}, bf16[1,1,768]{2,1,0:T(2,128)(2,1)S(1)}, u32[]{:S(2)}, u32[]{:S(2)}) collective-permute-start(bf16[1,1,768]{2,1,0:T(2,128)(2,1)S(1)} %get-tuple-element.24), channel_id=1, source_target_pairs={{0,1},{1,2},{2,3},{3,4},{4,5},{5,6},{6,7},{7,8},{8,9},{9,10},{10,1... | collective-permute-start | bytes 4616 | tf_op jit(solution)/shard_map/ppermute | solution.py:16
  17.5 29.4 %collective-permute-start.5 = (bf16[1,1,768]{2,1,0:T(2,128)(2,1)S(1)}, bf16[1,1,768]{2,1,0:T(2,128)(2,1)S(1)}, u32[]{:S(2)}, u32[]{:S(2)}) collective-permute-start(bf16[1,1,768]{2,1,0:T(2,128)(2,1)S(1)} %get-tuple-element.25), channel_id=1, source_target_pairs={{1,0},{2,1},{3,2},{4,3},{5,4},{6,5},{7,6},{8,7},{9,8},{10,9},{11,1... | collective-permute-start | bytes 4616 | tf_op jit(solution)/shard_map/ppermute | solution.py:17
  45.3 1.6 %copy-start.2 = (bf16[1,32,768]{2,1,0:T(8,128)(2,1)S(1)}, bf16[1,32,768]{2,1,0:T(8,128)(2,1)}, u32[]{:S(2)}) copy-start(bf16[1,32,768]{2,1,0:T(8,128)(2,1)} %param.11) | copy-start | bytes 147460
  45.4 1.9 %copy-start = (bf16[1,128,640]{2,1,0:T(8,128)(2,1)S(1)}, bf16[1,128,640]{2,1,0:T(8,128)(2,1)}, u32[]{:S(2)}) copy-start(bf16[1,128,640]{2,1,0:T(8,128)(2,1)} %param.6) | copy-start | bytes 491524
  46.2 1.9 %copy-start.4 = (f32[640]{0:T(1024)S(1)}, f32[640]{0:T(1024)}, u32[]{:S(2)}) copy-start(f32[640]{0:T(1024)} %param.7) | copy-start | bytes 7684
  47.2 0.8 copy-start.1
  51.7 7.8 %copy-start.3 = (f32[768]{0:T(1024)S(1)}, f32[768]{0:T(1024)}, u32[]{:S(2)}) copy-start(f32[768]{0:T(1024)} %param.9) | copy-start | bytes 9220
  52.2 7.0 %collective-permute-start.2 = (bf16[1,2,768]{2,1,0:T(2,128)(2,1)S(1)}, bf16[1,2,768]{2,1,0:T(2,128)(2,1)S(1)}, u32[]{:S(2)}, u32[]{:S(2)}) collective-permute-start(bf16[1,2,768]{2,1,0:T(2,128)(2,1)S(1)} %get-tuple-element.22), channel_id=1, source_target_pairs={{0,1},{1,2},{2,3},{3,4},{4,5},{5,6},{6,7},{7,8},{8,9},{9,10},{10,1... | collective-permute-start | bytes 9224 | tf_op jit(solution)/shard_map/ppermute | solution.py:16
  54.4 4.7 %collective-permute-start.3 = (bf16[1,2,768]{2,1,0:T(2,128)(2,1)S(1)}, bf16[1,2,768]{2,1,0:T(2,128)(2,1)S(1)}, u32[]{:S(2)}, u32[]{:S(2)}) collective-permute-start(bf16[1,2,768]{2,1,0:T(2,128)(2,1)S(1)} %get-tuple-element.23), channel_id=1, source_target_pairs={{1,0},{2,1},{3,2},{4,3},{5,4},{6,5},{7,6},{8,7},{9,8},{10,9},{11,1... | collective-permute-start | bytes 9224 | tf_op jit(solution)/shard_map/ppermute | solution.py:17
  73.3 50.3 %all-to-all-start.1 = ((bf16[16,2,1536]{2,1,0:T(2,128)(2,1)}), bf16[16,2,1536]{2,1,0:T(2,128)(2,1)S(1)}, u32[]{:S(2)}, u32[]{:S(2)}) async-start(bf16[16,2,1536]{2,1,0:T(2,128)(2,1)} %reshape.766), calls=%async_computation.1 | async-start | bytes 196608 | tf_op jit(solution)/shard_map/all_to_all | solution.py:83
  76.9 4.7 %collective-permute-start.6 = (bf16[1,1,768]{2,1,0:T(2,128)(2,1)S(1)}, bf16[1,1,768]{2,1,0:T(2,128)(2,1)S(1)}, u32[]{:S(2)}, u32[]{:S(2)}) collective-permute-start(bf16[1,1,768]{2,1,0:T(2,128)(2,1)S(1)} %get-tuple-element.20), channel_id=1, source_target_pairs={{0,1},{1,2},{2,3},{3,4},{4,5},{5,6},{6,7},{7,8},{8,9},{9,10},{10,1... | collective-permute-start | bytes 4616 | tf_op jit(solution)/shard_map/ppermute | solution.py:16
  79.7 3.8 %collective-permute-start.7 = (bf16[1,1,768]{2,1,0:T(2,128)(2,1)S(1)}, bf16[1,1,768]{2,1,0:T(2,128)(2,1)S(1)}, u32[]{:S(2)}, u32[]{:S(2)}) collective-permute-start(bf16[1,1,768]{2,1,0:T(2,128)(2,1)S(1)} %get-tuple-element.21), channel_id=1, source_target_pairs={{1,0},{2,1},{3,2},{4,3},{5,4},{6,5},{7,6},{8,7},{9,8},{10,9},{11,1... | collective-permute-start | bytes 4616 | tf_op jit(solution)/shard_map/ppermute | solution.py:17
  123.6 12.1 %all-to-all-start = ((bf16[16,2,2560]{2,1,0:T(2,128)(2,1)}), bf16[16,2,2560]{2,1,0:T(2,128)(2,1)S(1)}, u32[]{:S(2)}, u32[]{:S(2)}) async-start(bf16[16,2,2560]{2,1,0:T(2,128)(2,1)} %reshape.764), calls=%async_computation | async-start | bytes 327680 | tf_op jit(solution)/shard_map/all_to_all | solution.py:83
  150.6 0.8 copy-start.5
Sparse Core Ops, SparseCore 0:
  69.4 39.2 all-gather.1
where the time goes:
time: 159 us; the launch traced here: 158 us
  blocking collectives  60.1 us (38%)
  matrix products  25.4 us (16%)
  starting transfers between devices  25.1 us (16%)
  local copies, waits for them, and re-layouts  20.1 us (13%)
  between operations  14.6 us (9%)
  other arithmetic  9.57 us (6%)
  waiting for transfers between devices  3.44 us (2%)
    psum x1, blocking collectives, shards(): gain_totals = lax.psum((gain_first_part, gain_second_part), 'seq')  33.6 us
    all_gather x1, blocking collectives, weight_grads(): whole = lax.all_gather(cotangent, 'seq', axis=1, tiled=True)  26.5 us
    ppermute x4, starting transfers between devices, extended(): before = lax.ppermute(last, axis, up)  12.5 us
    broadcast_in_dim x4, local copies, waits for them, and re-layouts, weight_grads(): spread = jnp.repeat(whole, 2, axis=1) * 0.5  11.1 us
    dot_general x2, matrix products, backward_section(): lax.dot_general(stacked, weight, (((2,), (1,)), ((), ())), preferred_elem...  9.13 us
    dot_general x10, matrix products, weight_grads(): jnp.einsum('blc,blo->co', padded[:, k:k + length], spread, preferred_elem...  8.81 us
    dot_general x2, matrix products, forward_section(): projected = jnp.dot(hidden, weight, preferred_element_type=jnp.float32)  7.48 us
    all_to_all x2, starting transfers between devices, weight_grads(): lax.all_to_all(hidden_own, 'seq', split_axis=2, concat_axis=1, tiled=True)  7.34 us
  transfers between devices with their start and end apart: 11, of which 2 were waited for; matrix products, arithmetic and copies ran while one was open for 15% of the time, Pallas kernels for 0%

commit v1 on v0

v1 whole, which is shorter than its diff:
```python
import functools
import jax
import jax.numpy as jnp
from jax import lax
from jax.experimental import pallas as pl
from jax.experimental.pallas import tpu as pltpu
from jax.sharding import PartitionSpec as P

KERNEL = 5
GELU_A = 0.7978845608028654
GELU_B = 0.044715
HALO = 8
F32 = jnp.float32
BF16 = jnp.bfloat16


def round16(rows):
    return (rows + 15) // 16 * 16


def dot(a, b):
    return jnp.dot(a, b, preferred_element_type=F32)


def dot_t(a, b):
    return lax.dot_general(a, b, (((1,), (1,)), ((), ())), preferred_element_type=F32)


def mean_inverse(x):
    return lax.rsqrt(jnp.mean(x * x, axis=-1, keepdims=True) + 1e-06)


def gelu(x):
    return 0.5 * x * (1.0 + jnp.tanh(GELU_A * (x + GELU_B * x * x * x)))


def gelu_slope(x):
    t = jnp.tanh(GELU_A * (x + GELU_B * x * x * x))
    return 0.5 * (1.0 + t) + 0.5 * x * (1.0 - t * t) * GELU_A * (1.0 + 3.0 * GELU_B * x * x)


def picks(shape, test, value):
    row = lax.broadcasted_iota(jnp.int32, shape, 0)
    col = lax.broadcasted_iota(jnp.int32, shape, 1)
    return jnp.where(test(row, col), value, 0.0).astype(BF16)


def kernel(
    n, x_ref, g1_ref, w1_hbm, g2_ref, w2_hbm, up_ref,
    enc_ref, dx_ref, dw1_ref, dw2_ref, dg1_ref, dg2_ref,
    w1_ref, w2_ref, xl_ref, xr_ref, ul_ref, ur_ref,
    cbuf, ubuf, asend, arecv, gbuf,
    w_sem, halo_send, halo_recv, c_send, c_recv, u_send, u_recv, a_send, a_recv, g_send, g_recv,
):
    me = lax.axis_index("seq")
    own1, c0 = x_ref.shape[0], x_ref.shape[1] // 2
    own2, c2 = up_ref.shape
    c1 = g2_ref.shape[1]
    ext1, ext2 = own1 + 2 * HALO, own2 + 2 * HALO
    rows1, rows2 = c0 // n, c1 // n
    pad1, pad2 = round16(rows1), round16(rows2)
    outer = n // 4
    core = lax.rem(me, 2)
    mid_axis = lax.rem(me // 2, 2)
    far = me // 4

    def peer_id(index):
        return {"seq": index}

    barrier = pltpu.get_barrier_semaphore()

    def greet(d, _):
        pl.semaphore_signal(barrier, inc=1, device_id=peer_id(lax.rem(me + d, n)), device_id_type=pl.DeviceIdType.MESH)
        return 0

    lax.fori_loop(1, n, greet, 0)
    w1_copy = pltpu.make_async_copy(w1_hbm, w1_ref, w_sem.at[0])
    w2_copy = pltpu.make_async_copy(w2_hbm, w2_ref, w_sem.at[1])
    w2_copy.start()
    w1_copy.start()
    ubuf[me] = up_ref[...]
    pl.semaphore_wait(barrier, n - 1)

    def remote(src, dst, send, recv, index):
        return pltpu.make_async_remote_copy(
            src_ref=src, dst_ref=dst, send_sem=send, recv_sem=recv,
            device_id=peer_id(index), device_id_type=pl.DeviceIdType.MESH,
        )

    left, right = lax.rem(me + n - 1, n), lax.rem(me + 1, n)
    x_to_right = remote(x_ref.at[pl.ds(own1 - 16, 16)], xl_ref, halo_send.at[0], halo_recv.at[0], right)
    x_to_left = remote(x_ref.at[pl.ds(0, 16)], xr_ref, halo_send.at[1], halo_recv.at[1], left)
    u_to_right = remote(up_ref.at[pl.ds(own2 - 16, 16)], ul_ref, halo_send.at[2], halo_recv.at[2], right)
    u_to_left = remote(up_ref.at[pl.ds(0, 16)], ur_ref, halo_send.at[3], halo_recv.at[3], left)

    @pl.when(me < n - 1)
    def _():
        x_to_right.start()
        u_to_right.start()

    @pl.when(me > 0)
    def _():
        x_to_left.start()
        u_to_left.start()

    def slot(f, m, c):
        return (f * 2 + m) * 2 + c

    def gather_parts(buf, send, recv):
        def push(owner, target, k):
            return remote(buf.at[owner], buf.at[owner], send.at[k], recv.at[owner], target)

        def arrive(owner):
            push(owner, right, 0).wait_recv()

        along = [lax.rem(far + d, outer) for d in range(outer)]
        back = [lax.rem(far + outer - d, outer) for d in range(outer)]
        across = slot(far, 1 - mid_axis, core)
        twin = slot(far, mid_axis, 1 - core)

        def begin():
            push(me, across, 0).start()
            for d in range(1, outer):
                push(me, slot(along[d], mid_axis, core), d).start()
            push(me, twin, outer).start()

        def relay_far():
            for d in range(1, outer):
                owner = slot(back[d], mid_axis, core)
                arrive(owner)
                push(owner, across, outer + d).start()
                push(owner, twin, 2 * outer - 1 + d).start()

        def relay_across():
            for d in range(outer):
                owner = slot(back[d], 1 - mid_axis, core)
                arrive(owner)
                push(owner, twin, 3 * outer - 1 + d).start()

        def finish():
            for d in range(outer):
                for m in range(2):
                    arrive(slot(back[d], m, 1 - core))

        def drain():
            for k in range(n - 1):
                push(me, right, k).wait_send()

        return begin, relay_far, relay_across, finish, drain

    u_begin, u_far, u_across, u_finish, u_drain = gather_parts(ubuf, u_send, u_recv)
    c_begin, c_far, c_across, c_finish, c_drain = gather_parts(cbuf, c_send, c_recv)
    u_begin()

    @pl.when(me == 0)
    def _():
        xl_ref[...] = jnp.zeros_like(xl_ref)
        ul_ref[...] = jnp.zeros_like(ul_ref)

    @pl.when(me == n - 1)
    def _():
        xr_ref[...] = jnp.zeros_like(xr_ref)
        ur_ref[...] = jnp.zeros_like(ur_ref)

    @pl.when(me > 0)
    def _():
        x_to_right.wait_recv()
        u_to_right.wait_recv()

    @pl.when(me < n - 1)
    def _():
        x_to_left.wait_recv()
        u_to_left.wait_recv()

    gain1, gain2 = g1_ref[...], g2_ref[...]
    x = jnp.concatenate(
        [xl_ref[...].astype(F32)[16 - HALO :], x_ref[...].astype(F32), xr_ref[...].astype(F32)[:HALO]], axis=0
    )

    def activate(part):
        r = mean_inverse(part)
        return r, gelu(part * r * gain1).astype(BF16).astype(F32)

    xe, xo = x[:, :c0], x[:, c0:]
    _, ue = activate(xe)
    _, uo = activate(xo)
    pairs = 0.5 * (ue + uo)
    cross = 0.5 * (pltpu.roll(uo, 1, 0) + ue)
    w2_copy.wait()
    up = jnp.concatenate(
        [ul_ref[...].astype(F32)[16 - HALO :], up_ref[...].astype(F32), ur_ref[...].astype(F32)[:HALO]], axis=0
    ).astype(BF16)
    du2 = jnp.zeros((ext1, c1), F32)
    spread = None
    for k in range(KERNEL):
        pick = picks(
            (ext1, ext2),
            lambda i, r: (2 * r == i + HALO + 2 - k) | (2 * r + 1 == i + HALO + 2 - k),
            0.5,
        )
        part = dot(pick, up)
        if k == KERNEL // 2:
            spread = part
        du2 = du2 + dot_t(part.astype(BF16), w2_ref[:, k * c2 : (k + 1) * c2])

    w1_copy.wait()
    sources = [pltpu.roll(pairs, 1, 0), cross, pairs, pltpu.roll(cross, ext1 - 1, 0), pltpu.roll(pairs, ext1 - 1, 0)]
    conv = jnp.zeros((ext1, c1), F32)
    for k in range(KERNEL):
        conv = conv + dot(sources[k].astype(BF16), w1_ref[:, k * c1 : (k + 1) * c1])
    held = 0.5 * (xe + xo)
    if c1 > c0:
        held = jnp.concatenate([held, jnp.zeros((ext1, c1 - c0), F32)], axis=1)
    place = me * own1 - HALO + lax.broadcasted_iota(jnp.int32, (ext1, 1), 0)
    inside = (place >= 0) & (place < n * own1)
    mid = jnp.where(inside, conv + held, 0.0).astype(BF16)
    midf = mid.astype(F32)
    r2 = mean_inverse(midf)
    n2 = midf * r2 * gain2
    u2 = gelu(n2).astype(BF16)
    dn2 = du2 * gelu_slope(n2)
    terms2 = dn2 * midf * r2
    dg2 = jnp.sum(terms2[HALO : HALO + own1], axis=0, keepdims=True)
    h2 = dn2 * gain2
    dmid = r2 * h2 - midf * (r2 * r2 * r2) * jnp.mean(h2 * midf, axis=-1, keepdims=True) + spread
    dmid = jnp.where(inside, dmid, 0.0)
    cbuf[me] = dmid[HALO : HALO + own1].astype(BF16)
    dmid = dmid.astype(BF16)
    c_begin()

    columns1 = jnp.concatenate([ue[HALO : HALO + own1], uo[HALO : HALO + own1]], axis=0).T
    order = picks(
        (128, ext1),
        lambda t, i: ((t < own2) & (i == 2 * t + HALO)) | ((t >= own2) & (t < 2 * own2) & (i == 2 * (t - own2) + HALO + 1)),
        1.0,
    )
    columns2 = dot(order, u2).T
    for s in range(n):
        first = columns1[s * rows1 : (s + 1) * rows1]
        second = columns2[s * rows2 : (s + 1) * rows2]
        if pad1 > rows1:
            first = jnp.concatenate([first, jnp.zeros((pad1 - rows1, 128), F32)], axis=0)
        if pad2 > rows2:
            second = jnp.concatenate([second, jnp.zeros((pad2 - rows2, 128), F32)], axis=0)
        asend[s, 0:pad1, :] = first.astype(BF16)
        asend[s, pad1 : pad1 + pad2, :] = second.astype(BF16)
    arecv[me] = asend[me]

    def a_copy(d):
        target = lax.rem(me + d, n)
        return remote(asend.at[target], arecv.at[me], a_send.at[d], a_recv.at[me], target)

    def a_start(d, _):
        a_copy(d).start()
        return 0

    lax.fori_loop(1, n, a_start, 0)

    u_far()
    back = [dot_t(dmid, w1_ref[:, k * c1 : (k + 1) * c1]) for k in range(KERNEL)]
    ahead = slice(HALO + 1, HALO + 1 + own1)
    here = slice(HALO, HALO + own1)
    behind = slice(HALO - 1, HALO - 1 + own1)
    du_even = 0.5 * (back[0][ahead] + (back[1] + back[2])[here] + (back[3] + back[4])[behind])
    du_odd = 0.5 * ((back[0] + back[1])[ahead] + (back[2] + back[3])[here] + back[4][behind])
    skip = 0.5 * dmid.astype(F32)[here, :c0]
    dg1 = jnp.zeros((1, c0), F32)
    for side, du in ((0, du_even), (1, du_odd)):
        xs = x_ref[:, side * c0 : (side + 1) * c0].astype(F32)
        r = mean_inverse(xs)
        dn = du * gelu_slope(xs * r * gain1)
        dg1 = dg1 + jnp.sum(dn * xs * r, axis=0, keepdims=True)
        h = dn * gain1
        dx = r * h - xs * (r * r * r) * jnp.mean(h * xs, axis=-1, keepdims=True) + skip
        dx_ref[:, side * c0 : (side + 1) * c0] = dx.astype(BF16)
    gbuf[me] = jnp.concatenate([dg1, dg2], axis=1)

    def g_copy(d):
        target = lax.rem(me + d, n)
        return remote(gbuf.at[me], gbuf.at[me], g_send.at[d], g_recv.at[me], target)

    def g_start(d, _):
        g_copy(d).start()
        return 0

    c_far()
    lax.fori_loop(1, n, g_start, 0)
    u_across()

    enc = jnp.zeros((own2, c2), F32)
    for k in range(KERNEL):
        taps = picks(
            (own2, ext1),
            lambda m, i: (i == 2 * m + k - 2 + HALO) | (i == 2 * m + k - 1 + HALO),
            0.5,
        )
        enc = enc + dot(dot(taps, u2).astype(BF16), w2_ref[:, k * c2 : (k + 1) * c2])
    halves = picks((own2, ext1), lambda m, i: (i == 2 * m + HALO) | (i == 2 * m + 1 + HALO), 0.5)
    pooled = dot(halves, mid)
    if c2 > c1:
        pooled = jnp.concatenate([pooled, jnp.zeros((own2, c2 - c1), F32)], axis=1)
    enc_ref[...] = (enc + pooled).astype(BF16)

    c_across()

    def a_done(d, _):
        source = lax.rem(me + n - d, n)
        remote(asend.at[source], arecv.at[source], a_send.at[d], a_recv.at[source], source).wait_recv()
        return 0

    lax.fori_loop(1, n, a_done, 0)

    def taps_of(start, rows, length):
        group = 128 // length
        lane = lax.broadcasted_iota(jnp.int32, (rows, 128), 1)
        evens, odds = [], []
        for s in range(0, n, group):
            even = odd = jnp.zeros((rows, 128), F32)
            for g in range(group):
                block = arecv[s + g, start : start + rows, :].astype(F32)
                chosen = (lane >= g * length) & (lane < (g + 1) * length)
                shift = g * length
                even = jnp.where(chosen, pltpu.roll(block, shift, 1) if shift else block, even)
                shift = (g * length - length) % 128
                odd = jnp.where(chosen, pltpu.roll(block, shift, 1) if shift else block, odd)
            evens.append(even)
            odds.append(odd)
        even = jnp.concatenate(evens, axis=1)
        odd = jnp.concatenate(odds, axis=1)
        total = n * length
        lanes = lax.broadcasted_iota(jnp.int32, (rows, total), 1)

        def later(v):
            return jnp.where(lanes == 0, 0.0, pltpu.roll(v, 1, 1))

        def sooner(v):
            return jnp.where(lanes == total - 1, 0.0, pltpu.roll(v, total - 1, 1))

        pair = 0.5 * (even + odd)
        blocks = [later(pair), 0.5 * (later(odd) + even), pair, 0.5 * (odd + sooner(even)), sooner(pair)]
        return jnp.concatenate(blocks, axis=0).astype(BF16)

    u_finish()
    stack2 = taps_of(pad1, pad2, own2)
    grad2 = dot(stack2, ubuf[...].reshape(n * own2, c2))
    for k in range(KERNEL):
        dw2_ref[:, k * c2 : (k + 1) * c2] = grad2[k * pad2 : k * pad2 + rows2]
    stack1 = taps_of(0, pad1, own1)

    def g_done(d, _):
        source = lax.rem(me + n - d, n)
        remote(gbuf.at[source], gbuf.at[source], g_send.at[d], g_recv.at[source], source).wait_recv()
        return 0

    lax.fori_loop(1, n, g_done, 0)
    gains = jnp.sum(gbuf[...], axis=0)
    dg1_ref[...] = gains[:, :c0]
    dg2_ref[...] = gains[:, c0:]
    c_finish()
    grad1 = dot(stack1, cbuf[...].reshape(n * own1, c1))
    for k in range(KERNEL):
        dw1_ref[:, k * c1 : (k + 1) * c1] = grad1[k * pad1 : k * pad1 + rows1]

    @pl.when(me < n - 1)
    def _():
        x_to_right.wait_send()
        u_to_right.wait_send()

    @pl.when(me > 0)
    def _():
        x_to_left.wait_send()
        u_to_left.wait_send()

    u_drain()
    c_drain()

    def drain(d, _):
        a_copy(d).wait_send()
        g_copy(d).wait_send()
        return 0

    lax.fori_loop(1, n, drain, 0)


def shards(features, gain_first, weight_first, gain_second, weight_second, upstream):
    n = lax.axis_size("seq")
    length, c0 = features.shape[1:]
    own2, c2 = upstream.shape[1:]
    c1 = weight_second.shape[0]
    own1 = length // 2
    pads = round16(c0 // n) + round16(c1 // n)
    dma = pltpu.SemaphoreType.DMA
    vmem = pl.BlockSpec(memory_space=pltpu.VMEM)
    hbm = pl.BlockSpec(memory_space=pl.ANY)
    encoded, dx, dw1, dw2, dg1, dg2 = pl.pallas_call(
        functools.partial(kernel, n),
        out_shape=(
            jax.ShapeDtypeStruct((own2, c2), BF16),
            jax.ShapeDtypeStruct((own1, 2 * c0), BF16),
            jax.ShapeDtypeStruct((c0 // n, KERNEL * c1), F32),
            jax.ShapeDtypeStruct((c1 // n, KERNEL * c2), F32),
            jax.ShapeDtypeStruct((1, c0), F32),
            jax.ShapeDtypeStruct((1, c1), F32),
        ),
        in_specs=[vmem, vmem, hbm, vmem, hbm, vmem],
        out_specs=(vmem,) * 6,
        scratch_shapes=[
            pltpu.VMEM(weight_first.shape, BF16),
            pltpu.VMEM(weight_second.shape, BF16),
            pltpu.VMEM((16, 2 * c0), BF16),
            pltpu.VMEM((16, 2 * c0), BF16),
            pltpu.VMEM((16, c2), BF16),
            pltpu.VMEM((16, c2), BF16),
            pltpu.VMEM((n, own1, c1), BF16),
            pltpu.VMEM((n, own2, c2), BF16),
            pltpu.VMEM((n, pads, 128), BF16),
            pltpu.VMEM((n, pads, 128), BF16),
            pltpu.VMEM((n, 1, c0 + c1), F32),
            dma((2,)), dma((4,)), dma((4,)),
            dma((n,)), dma((n,)), dma((n,)), dma((n,)), dma((n,)), dma((n,)), dma((n,)), dma((n,)),
        ],
        compiler_params=pltpu.CompilerParams(
            collective_id=0, has_side_effects=True, vmem_limit_bytes=56 * 1024 * 1024
        ),
    )(
        features.reshape(own1, 2 * c0),
        gain_first[None],
        weight_first,
        gain_second[None],
        weight_second,
        upstream[0],
    )
    return (encoded[None], dx.reshape(1, length, c0), dw1, dw2, dg1[0], dg2[0])


def solution(mesh):
    placed = (P("groups", "seq", None), P(), P(), P(), P(), P("groups", "seq", None))
    return jax.shard_map(
        shards,
        mesh=mesh,
        in_specs=placed,
        out_specs=(
            P("groups", "seq", None),
            P("groups", "seq", None),
            P(("groups", "seq"), None),
            P(("groups", "seq"), None),
            P("groups"),
            P("groups"),
        ),
        check_vma=False,
    )
```

time: 159 us -> 53.9 us (0.34)
  blocking collectives: 60.1 us -> 0 us
  Pallas kernels: 0 us -> 39.1 us
  matrix products: 25.4 us -> 0 us
  starting transfers between devices: 25.1 us -> 0 us
  between operations: 14.6 us -> 0.64 us
  local copies, waits for them, and re-layouts: 20.1 us -> 11.2 us
  other arithmetic: 9.57 us -> 2.54 us
  waiting for transfers between devices: 3.44 us -> 0 us
    pallas_call x0 -> x1, Pallas kernels: none -> 39.1 us  [shards(): pl.pallas_call(functools.partial(kernel, n), out_shape=(jax.ShapeDtypeStr...]
    psum x1 -> x0, blocking collectives: 33.6 us -> none  [shards(): gain_totals = lax.psum((gain_first_part, gain_second_part), 'seq')]
    all_gather x1 -> x0, blocking collectives: 26.5 us -> none  [weight_grads(): whole = lax.all_gather(cotangent, 'seq', axis=1, tiled=True)]
    dot_general x14 -> x0, matrix products: 25.4 us -> none  [the longest x2 9.13 us: backward_section(): lax.dot_general(stacked, weight, (((2,), (1,)), ((), ())), preferred_elem...]
    ppermute x8 -> x0, starting transfers between devices: 17.7 us -> none  [the longest x4 12.5 us: extended(): before = lax.ppermute(last, axis, up)]
    broadcast_in_dim x6 -> x2, local copies, waits for them, and re-layouts: 11.2 us -> 2.53 us  [the longest x1 1.27 us: shards(): gain_second[None]]
    all_to_all x2 -> x0, starting transfers between devices: 7.34 us -> none  [weight_grads(): lax.all_to_all(hidden_own, 'seq', split_axis=2, concat_axis=1, tiled=True)]
    unnamed x2 -> x0, other arithmetic: 3.46 us -> none
  transfers between devices with their start and end apart: 11 -> 0, of which waited for: 2 -> 0; matrix products, arithmetic and copies ran while one was open for 15% -> 0% of each run, Pallas kernels for 0% -> 0%
where the time goes in v1:
time: 53.9 us; the launch traced here: 53.5 us
  Pallas kernels  39.1 us (73%)
  local copies, waits for them, and re-layouts  11.2 us (21%)
  other arithmetic  2.54 us (5%)
  between operations  0.64 us (1%)
    pallas_call x1, Pallas kernels, shards(): pl.pallas_call(functools.partial(kernel, n), out_shape=(jax.ShapeDtypeStr...  39.1 us
    unnamed x3, local copies, waits for them, and re-layouts  5.38 us
    pallas_call x2, other arithmetic, shards(): pl.pallas_call(functools.partial(kernel, n), out_shape=(jax.ShapeDtypeStr...  2.54 us
    reshape x1, local copies, waits for them, and re-layouts, shards(): return (encoded[None], dx.reshape(1, length, c0), dw1, dw2, dg1[0], dg2[0])  1.64 us
    reshape x1, local copies, waits for them, and re-layouts, shards(): features.reshape(own1, 2 * c0)  1.64 us
    broadcast_in_dim x1, local copies, waits for them, and re-layouts, shards(): gain_second[None]  1.27 us
    broadcast_in_dim x1, local copies, waits for them, and re-layouts, shards(): gain_first[None]  1.27 us

profile of v1, /device:TPU:0, one launch (start us, length us, event | category | flops | bytes accessed | tf_op | source)
XLA Modules:
  0.0 53.5 jit_solution(421880821645590740)
XLA Ops:
  0.6 1.6 %reshape.18.x_ref = bf16[64,1280]{1,0:T(8,128)(2,1)} reshape(bf16[1,128,640]{2,1,0:T(8,128)(2,1)} %param.6) | data formatting | bytes 327680 | tf_op jit(solution)/shard_map/reshape | solution.py:426
  2.3 1.3 %broadcast_in_dim.10.g2_ref = f32[1,768]{1,0:T(1,128)} reshape(f32[768]{0:T(1024)} %param.9) | data formatting | bytes 6144 | tf_op jit(solution)/shard_map/broadcast_in_dim | solution.py:429
  3.5 1.3 %broadcast_in_dim.9.g1_ref = f32[1,640]{1,0:T(1,128)} reshape(f32[640]{0:T(1024)} %param.7) | data formatting | bytes 5120 | tf_op jit(solution)/shard_map/broadcast_in_dim | solution.py:427
  4.8 39.1 %shard_map.109 = (bf16[32,768]{1,0:T(8,128)(2,1)}, bf16[64,1280]{1,0:T(8,128)(2,1)}, f32[40,3840]{1,0:T(8,128)}, f32[48,3840]{1,0:T(8,128)}, f32[1,640]{1,0:T(1,128)}, /*index=5*/f32[1,768]{1,0:T(1,128)}) custom-call(bf16[64,1280]{1,0:T(8,128)(2,1)} %reshape.18.x_ref, f32[1,640]{1,0:T(1,128)} %broadcast_in_dim.9.g1_ref, bf16[640,3840]{1,0:T(8,128)(2,1)} %w1_hbm.1, ...), custom_call_target="tpu_custom_call" | custom-call | tf_op jit(solution)/shard_map/pallas_call | solution.py:395
  43.9 1.6 %reshape.19 = bf16[1,128,640]{2,1,0:T(8,128)(2,1)} reshape(bf16[64,1280]{1,0:T(8,128)(2,1)} %get-tuple-element.13) | data formatting | bytes 327680 | tf_op jit(solution)/shard_map/reshape | solution.py:433
  45.6 1.3 %reduce = f32[640]{0:T(1024)} reduce(f32[1,640]{1,0:T(1,128)} %get-tuple-element.16, f32[]{:T(128)} %constant.2), dimensions={0}, to_apply=%get-tuple-element.16.reduce_sub_computation | reduce | bytes 5124 | tf_op jit(solution)/shard_map/pallas_call | solution.py:395
  46.8 1.3 %reduce.1 = f32[768]{0:T(1024)} reduce(f32[1,768]{1,0:T(1,128)} %get-tuple-element.17, f32[]{:T(128)} %constant.2), dimensions={0}, to_apply=%get-tuple-element.17.reduce_sub_computation | reduce | bytes 6148 | tf_op jit(solution)/shard_map/pallas_call | solution.py:395
  48.1 1.4 %copy.15 = bf16[1,32,768]{2,1,0:T(8,128)(2,1)} copy(bf16[1,32,768]{2,1,0:T(8,128)(2,1)} %bitcast.3) | data formatting | bytes 98304
  49.5 1.9 %copy.16 = f32[40,3840]{1,0:T(8,128)} copy(f32[40,3840]{1,0:T(8,128)} %get-tuple-element.26) | data formatting | bytes 1228800
  51.5 2.0 %copy.17 = f32[48,3840]{1,0:T(8,128)} copy(f32[48,3840]{1,0:T(8,128)} %get-tuple-element.27) | data formatting | bytes 1474560

commit v2 on v1

--- a/solution.py
+++ b/solution.py
@@ -53,9 +53,9 @@
     w_sem, halo_send, halo_recv, c_send, c_recv, u_send, u_recv, a_send, a_recv, g_send, g_recv,
 ):
     me = lax.axis_index("seq")
-    own1, c0 = x_ref.shape[0], x_ref.shape[1] // 2
-    own2, c2 = up_ref.shape
-    c1 = g2_ref.shape[1]
+    own1, c0 = x_ref.shape[1] // 2, x_ref.shape[2]
+    own2, c2 = up_ref.shape[1:]
+    c1 = g2_ref.shape[0]
     ext1, ext2 = own1 + 2 * HALO, own2 + 2 * HALO
     rows1, rows2 = c0 // n, c1 // n
     pad1, pad2 = round16(rows1), round16(rows2)
@@ -78,7 +78,7 @@
     w2_copy = pltpu.make_async_copy(w2_hbm, w2_ref, w_sem.at[1])
     w2_copy.start()
     w1_copy.start()
-    ubuf[me] = up_ref[...]
+    ubuf[me] = up_ref[0]
     pl.semaphore_wait(barrier, n - 1)
 
     def remote(src, dst, send, recv, index):
@@ -88,10 +88,10 @@
         )
 
     left, right = lax.rem(me + n - 1, n), lax.rem(me + 1, n)
-    x_to_right = remote(x_ref.at[pl.ds(own1 - 16, 16)], xl_ref, halo_send.at[0], halo_recv.at[0], right)
-    x_to_left = remote(x_ref.at[pl.ds(0, 16)], xr_ref, halo_send.at[1], halo_recv.at[1], left)
-    u_to_right = remote(up_ref.at[pl.ds(own2 - 16, 16)], ul_ref, halo_send.at[2], halo_recv.at[2], right)
-    u_to_left = remote(up_ref.at[pl.ds(0, 16)], ur_ref, halo_send.at[3], halo_recv.at[3], left)
+    x_to_right = remote(x_ref.at[0, pl.ds(2 * own1 - 16, 16)], xl_ref, halo_send.at[0], halo_recv.at[0], right)
+    x_to_left = remote(x_ref.at[0, pl.ds(0, 16)], xr_ref, halo_send.at[1], halo_recv.at[1], left)
+    u_to_right = remote(up_ref.at[0, pl.ds(own2 - 16, 16)], ul_ref, halo_send.at[2], halo_recv.at[2], right)
+    u_to_left = remote(up_ref.at[0, pl.ds(0, 16)], ur_ref, halo_send.at[3], halo_recv.at[3], left)
 
     @pl.when(me < n - 1)
     def _():
@@ -172,23 +172,22 @@
         x_to_left.wait_recv()
         u_to_left.wait_recv()
 
-    gain1, gain2 = g1_ref[...], g2_ref[...]
-    x = jnp.concatenate(
-        [xl_ref[...].astype(F32)[16 - HALO :], x_ref[...].astype(F32), xr_ref[...].astype(F32)[:HALO]], axis=0
-    )
+    gain1, gain2 = g1_ref[...].reshape(1, c0), g2_ref[...].reshape(1, c1)
+    x = jnp.concatenate([xl_ref[...], x_ref[0], xr_ref[...]], axis=0)
 
     def activate(part):
         r = mean_inverse(part)
         return r, gelu(part * r * gain1).astype(BF16).astype(F32)
 
-    xe, xo = x[:, :c0], x[:, c0:]
+    xe = dot(picks((ext1, 2 * ext1), lambda j, i: i == 2 * j, 1.0), x)
+    xo = dot(picks((ext1, 2 * ext1), lambda j, i: i == 2 * j + 1, 1.0), x)
     _, ue = activate(xe)
     _, uo = activate(xo)
     pairs = 0.5 * (ue + uo)
     cross = 0.5 * (pltpu.roll(uo, 1, 0) + ue)
     w2_copy.wait()
     up = jnp.concatenate(
-        [ul_ref[...].astype(F32)[16 - HALO :], up_ref[...].astype(F32), ur_ref[...].astype(F32)[:HALO]], axis=0
+        [ul_ref[...].astype(F32)[16 - HALO :], up_ref[0].astype(F32), ur_ref[...].astype(F32)[:HALO]], axis=0
     ).astype(BF16)
     du2 = jnp.zeros((ext1, c1), F32)
     spread = None
@@ -265,14 +264,18 @@
     du_odd = 0.5 * ((back[0] + back[1])[ahead] + (back[2] + back[3])[here] + back[4][behind])
     skip = 0.5 * dmid.astype(F32)[here, :c0]
     dg1 = jnp.zeros((1, c0), F32)
-    for side, du in ((0, du_even), (1, du_odd)):
-        xs = x_ref[:, side * c0 : (side + 1) * c0].astype(F32)
+    sides = []
+    for ext, du in ((xe, du_even), (xo, du_odd)):
+        xs = ext[here]
         r = mean_inverse(xs)
         dn = du * gelu_slope(xs * r * gain1)
         dg1 = dg1 + jnp.sum(dn * xs * r, axis=0, keepdims=True)
         h = dn * gain1
         dx = r * h - xs * (r * r * r) * jnp.mean(h * xs, axis=-1, keepdims=True) + skip
-        dx_ref[:, side * c0 : (side + 1) * c0] = dx.astype(BF16)
+        sides.append(dx.astype(BF16))
+    weave_even = picks((2 * own1, own1), lambda i, j: i == 2 * j, 1.0)
+    weave_odd = picks((2 * own1, own1), lambda i, j: i == 2 * j + 1, 1.0)
+    dx_ref[0] = (dot(weave_even, sides[0]) + dot(weave_odd, sides[1])).astype(BF16)
     gbuf[me] = jnp.concatenate([dg1, dg2], axis=1)
 
     def g_copy(d):
@@ -299,7 +302,7 @@
     pooled = dot(halves, mid)
     if c2 > c1:
         pooled = jnp.concatenate([pooled, jnp.zeros((own2, c2 - c1), F32)], axis=1)
-    enc_ref[...] = (enc + pooled).astype(BF16)
+    enc_ref[0] = (enc + pooled).astype(BF16)
 
     c_across()
 
@@ -354,8 +357,8 @@
 
     lax.fori_loop(1, n, g_done, 0)
     gains = jnp.sum(gbuf[...], axis=0)
-    dg1_ref[...] = gains[:, :c0]
-    dg2_ref[...] = gains[:, c0:]
+    dg1_ref[...] = gains[:, :c0].reshape(c0)
+    dg2_ref[...] = gains[:, c0:].reshape(c1)
     c_finish()
     grad1 = dot(stack1, cbuf[...].reshape(n * own1, c1))
     for k in range(KERNEL):
@@ -380,6 +383,16 @@
         return 0
 
     lax.fori_loop(1, n, drain, 0)
+
+
+def place_results(*refs):
+    count = len(refs) // 2
+    sems = refs[-1]
+    copies = [pltpu.make_async_copy(refs[i], refs[count + i], sems.at[i]) for i in range(count)]
+    for copy in copies:
+        copy.start()
+    for copy in copies:
+        copy.wait()
 
 
 def shards(features, gain_first, weight_first, gain_second, weight_second, upstream):
@@ -392,23 +405,23 @@
     dma = pltpu.SemaphoreType.DMA
     vmem = pl.BlockSpec(memory_space=pltpu.VMEM)
     hbm = pl.BlockSpec(memory_space=pl.ANY)
-    encoded, dx, dw1, dw2, dg1, dg2 = pl.pallas_call(
+    results = pl.pallas_call(
         functools.partial(kernel, n),
         out_shape=(
-            jax.ShapeDtypeStruct((own2, c2), BF16),
-            jax.ShapeDtypeStruct((own1, 2 * c0), BF16),
+            jax.ShapeDtypeStruct((1, own2, c2), BF16),
+            jax.ShapeDtypeStruct((1, length, c0), BF16),
             jax.ShapeDtypeStruct((c0 // n, KERNEL * c1), F32),
             jax.ShapeDtypeStruct((c1 // n, KERNEL * c2), F32),
-            jax.ShapeDtypeStruct((1, c0), F32),
-            jax.ShapeDtypeStruct((1, c1), F32),
+            jax.ShapeDtypeStruct((c0,), F32),
+            jax.ShapeDtypeStruct((c1,), F32),
         ),
         in_specs=[vmem, vmem, hbm, vmem, hbm, vmem],
         out_specs=(vmem,) * 6,
         scratch_shapes=[
             pltpu.VMEM(weight_first.shape, BF16),
             pltpu.VMEM(weight_second.shape, BF16),
-            pltpu.VMEM((16, 2 * c0), BF16),
-            pltpu.VMEM((16, 2 * c0), BF16),
+            pltpu.VMEM((16, c0), BF16),
+            pltpu.VMEM((16, c0), BF16),
             pltpu.VMEM((16, c2), BF16),
             pltpu.VMEM((16, c2), BF16),
             pltpu.VMEM((n, own1, c1), BF16),
@@ -423,14 +436,20 @@
             collective_id=0, has_side_effects=True, vmem_limit_bytes=56 * 1024 * 1024
         ),
     )(
-        features.reshape(own1, 2 * c0),
-        gain_first[None],
+        features,
+        gain_first,
         weight_first,
-        gain_second[None],
+        gain_second,
         weight_second,
-        upstream[0],
+        upstream,
     )
-    return (encoded[None], dx.reshape(1, length, c0), dw1, dw2, dg1[0], dg2[0])
+    return pl.pallas_call(
+        place_results,
+        out_shape=tuple(jax.ShapeDtypeStruct(r.shape, r.dtype) for r in results),
+        in_specs=[hbm] * len(results),
+        out_specs=(hbm,) * len(results),
+        scratch_shapes=[dma((len(results),))],
+    )(*results)
 
 
 def solution(mesh):

time: 53.9 us -> 88.4 us (1.64)
  Pallas kernels: 39.1 us -> 87.6 us
  local copies, waits for them, and re-layouts: 11.2 us -> 0 us
  other arithmetic: 2.54 us -> 0 us
    pallas_call x0 -> x1, Pallas kernels: none -> 48.7 us  [shards(): pl.pallas_call(place_results, out_shape=tuple((jax.ShapeDtypeStruct(r.sha...]
    unnamed x3 -> x0, local copies, waits for them, and re-layouts: 5.38 us -> none
    reshape x2 -> x0, local copies, waits for them, and re-layouts: 3.28 us -> none  [the longest x1 1.64 us: shards(): return (encoded[None], dx.reshape(1, length, c0), dw1, dw2, dg1[0], dg2[0])]
    pallas_call x2 -> x0, other arithmetic: 2.54 us -> none  [shards(): pl.pallas_call(functools.partial(kernel, n), out_shape=(jax.ShapeDtypeStr...]
    broadcast_in_dim x2 -> x0, local copies, waits for them, and re-layouts: 2.53 us -> none  [the longest x1 1.27 us: shards(): gain_second[None]]
where the time goes in v2:
time: 88.4 us; the launch traced here: 88.2 us
  Pallas kernels  87.6 us (99%)
    pallas_call x1, Pallas kernels, shards(): pl.pallas_call(place_results, out_shape=tuple((jax.ShapeDtypeStruct(r.sha...  48.7 us
    pallas_call x1, Pallas kernels, shards(): pl.pallas_call(functools.partial(kernel, n), out_shape=(jax.ShapeDtypeStr...  38.9 us

profile of v2, /device:TPU:0, one launch (start us, length us, event | category | flops | bytes accessed | tf_op | source)
XLA Modules:
  0.0 88.2 jit_solution(3036280424023734818)
XLA Ops:
  0.6 38.9 %shard_map.109 = (bf16[1,32,768]{2,1,0:T(8,128)(2,1)}, bf16[1,128,640]{2,1,0:T(8,128)(2,1)}, f32[40,3840]{1,0:T(8,128)}, f32[48,3840]{1,0:T(8,128)}, f32[640]{0:T(1024)}, /*index=5*/f32[768]{0:T(1024)}) custom-call(bf16[1,128,640]{2,1,0:T(8,128)(2,1)} %x_ref.1, f32[640]{0:T(1024)} %g1_ref.1, bf16[640,3840]{1,0:T(8,128)(2,1)} %w1_hbm.1, f32[768]{0:T(1024)} %g2_ref.1, ...), custom_call_target="tpu_custom_call" | custom-call | tf_op jit(solution)/shard_map/pallas_call | solution.py:408
  39.5 48.7 %shard_map.110 = (bf16[1,32,768]{2,1,0:T(8,128)(2,1)}, bf16[1,128,640]{2,1,0:T(8,128)(2,1)}, f32[40,3840]{1,0:T(8,128)}, f32[48,3840]{1,0:T(8,128)}, f32[640]{0:T(1024)}, /*index=5*/f32[768]{0:T(1024)}) custom-call(bf16[1,32,768]{2,1,0:T(8,128)(2,1)} %get-tuple-element.12.refs_0_, bf16[1,128,640]{2,1,0:T(8,128)(2,1)} %get-tuple-element.13.refs_1_, ...), custom_call_target="tpu_custom_call" | custom-call | tf_op jit(solution)/shard_map/pallas_call | solution.py:446

commit v3 on v2

--- a/solution.py
+++ b/solution.py
@@ -49,8 +49,8 @@
     n, x_ref, g1_ref, w1_hbm, g2_ref, w2_hbm, up_ref,
     enc_ref, dx_ref, dw1_ref, dw2_ref, dg1_ref, dg2_ref,
     w1_ref, w2_ref, xl_ref, xr_ref, ul_ref, ur_ref,
-    cbuf, ubuf, asend, arecv, gbuf,
-    w_sem, halo_send, halo_recv, c_send, c_recv, u_send, u_recv, a_send, a_recv, g_send, g_recv,
+    cbuf, ubuf, asend1, arecv1, asend2, arecv2, gbuf,
+    w_sem, halo_send, halo_recv, c_send, c_recv, u_send, u_recv, a_send, a_recv, b_send, b_recv, g_send, g_recv,
 ):
     me = lax.axis_index("seq")
     own1, c0 = x_ref.shape[1] // 2, x_ref.shape[2]
@@ -185,6 +185,30 @@
     _, uo = activate(xo)
     pairs = 0.5 * (ue + uo)
     cross = 0.5 * (pltpu.roll(uo, 1, 0) + ue)
+    columns1 = jnp.concatenate([ue[HALO : HALO + own1], uo[HALO : HALO + own1]], axis=0).T
+    for s in range(n):
+        asend1[s] = columns1[s * rows1 : (s + 1) * rows1].astype(BF16)
+    arecv1[me] = asend1[me]
+
+    def exchange(sent, received, send, recv):
+        def copy(d):
+            target = lax.rem(me + d, n)
+            return remote(sent.at[target], received.at[me], send.at[d], recv.at[me], target)
+
+        def start(d, _):
+            copy(d).start()
+            return 0
+
+        def arrive(d, _):
+            source = lax.rem(me + n - d, n)
+            remote(sent.at[source], received.at[source], send.at[d], recv.at[source], source).wait_recv()
+            return 0
+
+        return copy, start, arrive
+
+    a_copy, a_start, a_done = exchange(asend1, arecv1, a_send, a_recv)
+    b_copy, b_start, b_done = exchange(asend2, arecv2, b_send, b_recv)
+    lax.fori_loop(1, n, a_start, 0)
     w2_copy.wait()
     up = jnp.concatenate(
         [ul_ref[...].astype(F32)[16 - HALO :], up_ref[0].astype(F32), ur_ref[...].astype(F32)[:HALO]], axis=0
@@ -202,11 +226,13 @@
             spread = part
         du2 = du2 + dot_t(part.astype(BF16), w2_ref[:, k * c2 : (k + 1) * c2])
 
+    u_far()
     w1_copy.wait()
     sources = [pltpu.roll(pairs, 1, 0), cross, pairs, pltpu.roll(cross, ext1 - 1, 0), pltpu.roll(pairs, ext1 - 1, 0)]
     conv = jnp.zeros((ext1, c1), F32)
     for k in range(KERNEL):
         conv = conv + dot(sources[k].astype(BF16), w1_ref[:, k * c1 : (k + 1) * c1])
+    u_across()
     held = 0.5 * (xe + xo)
     if c1 > c0:
         held = jnp.concatenate([held, jnp.zeros((ext1, c1 - c0), F32)], axis=1)
@@ -227,35 +253,21 @@
     dmid = dmid.astype(BF16)
     c_begin()
 
-    columns1 = jnp.concatenate([ue[HALO : HALO + own1], uo[HALO : HALO + own1]], axis=0).T
     order = picks(
         (128, ext1),
-        lambda t, i: ((t < own2) & (i == 2 * t + HALO)) | ((t >= own2) & (t < 2 * own2) & (i == 2 * (t - own2) + HALO + 1)),
+        lambda t, i: ((t % 64 < own2) & (i == 2 * (t % 64) + HALO))
+        | ((t % 64 >= own2) & (i == 2 * (t % 64 - own2) + HALO + 1)),
         1.0,
     )
     columns2 = dot(order, u2).T
+    low = lax.broadcasted_iota(jnp.int32, (rows2 // 2, 128), 1) < 64
     for s in range(n):
-        first = columns1[s * rows1 : (s + 1) * rows1]
-        second = columns2[s * rows2 : (s + 1) * rows2]
-        if pad1 > rows1:
-            first = jnp.concatenate([first, jnp.zeros((pad1 - rows1, 128), F32)], axis=0)
-        if pad2 > rows2:
-            second = jnp.concatenate([second, jnp.zeros((pad2 - rows2, 128), F32)], axis=0)
-        asend[s, 0:pad1, :] = first.astype(BF16)
-        asend[s, pad1 : pad1 + pad2, :] = second.astype(BF16)
-    arecv[me] = asend[me]
-
-    def a_copy(d):
-        target = lax.rem(me + d, n)
-        return remote(asend.at[target], arecv.at[me], a_send.at[d], a_recv.at[me], target)
-
-    def a_start(d, _):
-        a_copy(d).start()
-        return 0
-
-    lax.fori_loop(1, n, a_start, 0)
-
-    u_far()
+        top = columns2[s * rows2 : s * rows2 + rows2 // 2]
+        bottom = columns2[s * rows2 + rows2 // 2 : (s + 1) * rows2]
+        asend2[s] = jnp.where(low, top, bottom).astype(BF16)
+    arecv2[me] = asend2[me]
+    lax.fori_loop(1, n, b_start, 0)
+
     back = [dot_t(dmid, w1_ref[:, k * c1 : (k + 1) * c1]) for k in range(KERNEL)]
     ahead = slice(HALO + 1, HALO + 1 + own1)
     here = slice(HALO, HALO + own1)
@@ -276,20 +288,21 @@
     weave_even = picks((2 * own1, own1), lambda i, j: i == 2 * j, 1.0)
     weave_odd = picks((2 * own1, own1), lambda i, j: i == 2 * j + 1, 1.0)
     dx_ref[0] = (dot(weave_even, sides[0]) + dot(weave_odd, sides[1])).astype(BF16)
-    gbuf[me] = jnp.concatenate([dg1, dg2], axis=1)
-
-    def g_copy(d):
-        target = lax.rem(me + d, n)
-        return remote(gbuf.at[me], gbuf.at[me], g_send.at[d], g_recv.at[me], target)
-
-    def g_start(d, _):
-        g_copy(d).start()
-        return 0
-
+    twin = slot(far, mid_axis, 1 - core)
+    across = slot(far, 1 - mid_axis, core)
+    gain_twin = remote(gbuf.at[0], gbuf.at[1], g_send.at[0], g_recv.at[0], twin)
+    gain_across = remote(gbuf.at[2], gbuf.at[3], g_send.at[1], g_recv.at[1], across)
+
+    def gain_far(d, sign):
+        other = lax.rem(far + outer + sign * d, outer)
+        owner = far if sign > 0 else other
+        return remote(
+            gbuf.at[4 + owner], gbuf.at[4 + owner], g_send.at[1 + d], g_recv.at[2 + owner], slot(other, mid_axis, core)
+        )
+
+    gbuf[0] = jnp.concatenate([dg1, dg2], axis=1)
+    gain_twin.start()
     c_far()
-    lax.fori_loop(1, n, g_start, 0)
-    u_across()
-
     enc = jnp.zeros((own2, c2), F32)
     for k in range(KERNEL):
         taps = picks(
@@ -304,23 +317,19 @@
         pooled = jnp.concatenate([pooled, jnp.zeros((own2, c2 - c1), F32)], axis=1)
     enc_ref[0] = (enc + pooled).astype(BF16)
 
+    gain_twin.wait_recv()
+    gbuf[2] = gbuf[0] + gbuf[1]
+    gain_across.start()
     c_across()
 
-    def a_done(d, _):
-        source = lax.rem(me + n - d, n)
-        remote(asend.at[source], arecv.at[source], a_send.at[d], a_recv.at[source], source).wait_recv()
-        return 0
-
-    lax.fori_loop(1, n, a_done, 0)
-
-    def taps_of(start, rows, length):
+    def taps_of(read, rows, length):
         group = 128 // length
         lane = lax.broadcasted_iota(jnp.int32, (rows, 128), 1)
         evens, odds = [], []
         for s in range(0, n, group):
             even = odd = jnp.zeros((rows, 128), F32)
             for g in range(group):
-                block = arecv[s + g, start : start + rows, :].astype(F32)
+                block = read(s + g)
                 chosen = (lane >= g * length) & (lane < (g + 1) * length)
                 shift = g * length
                 even = jnp.where(chosen, pltpu.roll(block, shift, 1) if shift else block, even)
@@ -343,20 +352,30 @@
         blocks = [later(pair), 0.5 * (later(odd) + even), pair, 0.5 * (odd + sooner(even)), sooner(pair)]
         return jnp.concatenate(blocks, axis=0).astype(BF16)
 
+    def padded(block, rows):
+        if rows == block.shape[0]:
+            return block
+        return jnp.concatenate([block, jnp.zeros((rows - block.shape[0], 128), F32)], axis=0)
+
+    def unfolded(s):
+        block = arecv2[s].astype(F32)
+        return padded(jnp.concatenate([block, pltpu.roll(block, 64, 1)], axis=0), pad2)
+
+    lax.fori_loop(1, n, a_done, 0)
+    stack1 = taps_of(lambda s: padded(arecv1[s].astype(F32), pad1), pad1, own1)
+    gain_across.wait_recv()
+    gbuf[4 + far] = gbuf[2] + gbuf[3]
+    for d in range(1, outer):
+        gain_far(d, 1).start()
     u_finish()
-    stack2 = taps_of(pad1, pad2, own2)
+    lax.fori_loop(1, n, b_done, 0)
+    stack2 = taps_of(unfolded, pad2, own2)
     grad2 = dot(stack2, ubuf[...].reshape(n * own2, c2))
     for k in range(KERNEL):
         dw2_ref[:, k * c2 : (k + 1) * c2] = grad2[k * pad2 : k * pad2 + rows2]
-    stack1 = taps_of(0, pad1, own1)
-
-    def g_done(d, _):
-        source = lax.rem(me + n - d, n)
-        remote(gbuf.at[source], gbuf.at[source], g_send.at[d], g_recv.at[source], source).wait_recv()
-        return 0
-
-    lax.fori_loop(1, n, g_done, 0)
-    gains = jnp.sum(gbuf[...], axis=0)
+    for d in range(1, outer):
+        gain_far(d, -1).wait_recv()
+    gains = jnp.sum(gbuf[4 : 4 + outer], axis=0)
     dg1_ref[...] = gains[:, :c0].reshape(c0)
     dg2_ref[...] = gains[:, c0:].reshape(c1)
     c_finish()
@@ -376,10 +395,14 @@
 
     u_drain()
     c_drain()
+    gain_twin.wait_send()
+    gain_across.wait_send()
+    for d in range(1, outer):
+        gain_far(d, 1).wait_send()
 
     def drain(d, _):
         a_copy(d).wait_send()
-        g_copy(d).wait_send()
+        b_copy(d).wait_send()
         return 0
 
     lax.fori_loop(1, n, drain, 0)
@@ -401,7 +424,6 @@
     own2, c2 = upstream.shape[1:]
     c1 = weight_second.shape[0]
     own1 = length // 2
-    pads = round16(c0 // n) + round16(c1 // n)
     dma = pltpu.SemaphoreType.DMA
     vmem = pl.BlockSpec(memory_space=pltpu.VMEM)
     hbm = pl.BlockSpec(memory_space=pl.ANY)
@@ -426,11 +448,14 @@
             pltpu.VMEM((16, c2), BF16),
             pltpu.VMEM((n, own1, c1), BF16),
             pltpu.VMEM((n, own2, c2), BF16),
-            pltpu.VMEM((n, pads, 128), BF16),
-            pltpu.VMEM((n, pads, 128), BF16),
-            pltpu.VMEM((n, 1, c0 + c1), F32),
+            pltpu.VMEM((n, c0 // n, 128), BF16),
+            pltpu.VMEM((n, c0 // n, 128), BF16),
+            pltpu.VMEM((n, c1 // n // 2, 128), BF16),
+            pltpu.VMEM((n, c1 // n // 2, 128), BF16),
+            pltpu.VMEM((4 + n // 4, 1, c0 + c1), F32),
             dma((2,)), dma((4,)), dma((4,)),
             dma((n,)), dma((n,)), dma((n,)), dma((n,)), dma((n,)), dma((n,)), dma((n,)), dma((n,)),
+            dma((1 + n // 4,)), dma((2 + n // 4,)),
         ],
         compiler_params=pltpu.CompilerParams(
             collective_id=0, has_side_effects=True, vmem_limit_bytes=56 * 1024 * 1024
@@ -446,7 +471,7 @@
     return pl.pallas_call(
         place_results,
         out_shape=tuple(jax.ShapeDtypeStruct(r.shape, r.dtype) for r in results),
-        in_specs=[hbm] * len(results),
+        in_specs=[vmem] * len(results),
         out_specs=(hbm,) * len(results),
         scratch_shapes=[dma((len(results),))],
     )(*results)

time: 88.4 us -> 46.8 us (0.53)
  Pallas kernels: 87.6 us -> 45.9 us
    pallas_call x1, Pallas kernels: 48.7 us -> 2.6 us  [shards(): pl.pallas_call(place_results, out_shape=tuple((jax.ShapeDtypeStruct(r.sha...]
    pallas_call x1, Pallas kernels: 38.9 us -> 43.3 us  [shards(): pl.pallas_call(functools.partial(kernel, n), out_shape=(jax.ShapeDtypeStr...]
where the time goes in v3:
time: 46.8 us; the launch traced here: 46.6 us
  Pallas kernels  45.9 us (98%)
  between operations  0.64 us (1%)
    pallas_call x1, Pallas kernels, shards(): pl.pallas_call(functools.partial(kernel, n), out_shape=(jax.ShapeDtypeStr...  43.3 us
    pallas_call x1, Pallas kernels, shards(): pl.pallas_call(place_results, out_shape=tuple((jax.ShapeDtypeStruct(r.sha...  2.6 us

profile of v3, /device:TPU:0, one launch (start us, length us, event | category | flops | bytes accessed | tf_op | source)
XLA Modules:
  0.0 46.6 jit_solution(8777492480165626412)
XLA Ops:
  0.6 43.3 %shard_map.109 = (bf16[1,32,768]{2,1,0:T(8,128)(2,1)}, bf16[1,128,640]{2,1,0:T(8,128)(2,1)}, f32[40,3840]{1,0:T(8,128)}, f32[48,3840]{1,0:T(8,128)}, f32[640]{0:T(1024)}, /*index=5*/f32[768]{0:T(1024)}) custom-call(bf16[1,128,640]{2,1,0:T(8,128)(2,1)} %x_ref.1, f32[640]{0:T(1024)} %g1_ref.1, bf16[640,3840]{1,0:T(8,128)(2,1)} %w1_hbm.1, f32[768]{0:T(1024)} %g2_ref.1, ...), custom_call_target="tpu_custom_call" | custom-call | tf_op jit(solution)/shard_map/pallas_call | solution.py:430
  44.0 2.6 %shard_map.110 = (bf16[1,32,768]{2,1,0:T(8,128)(2,1)}, bf16[1,128,640]{2,1,0:T(8,128)(2,1)}, f32[40,3840]{1,0:T(8,128)}, f32[48,3840]{1,0:T(8,128)}, f32[640]{0:T(1024)}, /*index=5*/f32[768]{0:T(1024)}) custom-call(bf16[1,32,768]{2,1,0:T(8,128)(2,1)} %get-tuple-element.12.refs_0_, bf16[1,128,640]{2,1,0:T(8,128)(2,1)} %get-tuple-element.13.refs_1_, ...), custom_call_target="tpu_custom_call" | custom-call | tf_op jit(solution)/shard_map/pallas_call | solution.py:471

commit v4 on v3

--- a/solution.py
+++ b/solution.py
@@ -113,6 +113,7 @@
         def arrive(owner):
             push(owner, right, 0).wait_recv()
 
+        nearest = sorted(range(1, outer), key=lambda d: min(d, outer - d))
         along = [lax.rem(far + d, outer) for d in range(outer)]
         back = [lax.rem(far + outer - d, outer) for d in range(outer)]
         across = slot(far, 1 - mid_axis, core)
@@ -120,19 +121,19 @@
 
         def begin():
             push(me, across, 0).start()
-            for d in range(1, outer):
+            for d in nearest:
                 push(me, slot(along[d], mid_axis, core), d).start()
             push(me, twin, outer).start()
 
         def relay_far():
-            for d in range(1, outer):
+            for d in nearest:
                 owner = slot(back[d], mid_axis, core)
                 arrive(owner)
                 push(owner, across, outer + d).start()
                 push(owner, twin, 2 * outer - 1 + d).start()
 
         def relay_across():
-            for d in range(outer):
+            for d in [0] + nearest:
                 owner = slot(back[d], 1 - mid_axis, core)
                 arrive(owner)
                 push(owner, twin, 3 * outer - 1 + d).start()
@@ -226,13 +227,11 @@
             spread = part
         du2 = du2 + dot_t(part.astype(BF16), w2_ref[:, k * c2 : (k + 1) * c2])
 
-    u_far()
     w1_copy.wait()
     sources = [pltpu.roll(pairs, 1, 0), cross, pairs, pltpu.roll(cross, ext1 - 1, 0), pltpu.roll(pairs, ext1 - 1, 0)]
     conv = jnp.zeros((ext1, c1), F32)
     for k in range(KERNEL):
         conv = conv + dot(sources[k].astype(BF16), w1_ref[:, k * c1 : (k + 1) * c1])
-    u_across()
     held = 0.5 * (xe + xo)
     if c1 > c0:
         held = jnp.concatenate([held, jnp.zeros((ext1, c1 - c0), F32)], axis=1)
@@ -266,7 +265,7 @@
         bottom = columns2[s * rows2 + rows2 // 2 : (s + 1) * rows2]
         asend2[s] = jnp.where(low, top, bottom).astype(BF16)
     arecv2[me] = asend2[me]
-    lax.fori_loop(1, n, b_start, 0)
+    u_far()
 
     back = [dot_t(dmid, w1_ref[:, k * c1 : (k + 1) * c1]) for k in range(KERNEL)]
     ahead = slice(HALO + 1, HALO + 1 + own1)
@@ -303,6 +302,11 @@
     gbuf[0] = jnp.concatenate([dg1, dg2], axis=1)
     gain_twin.start()
     c_far()
+    lax.fori_loop(1, n, b_start, 0)
+    gain_twin.wait_recv()
+    gbuf[2] = gbuf[0] + gbuf[1]
+    gain_across.start()
+    u_across()
     enc = jnp.zeros((own2, c2), F32)
     for k in range(KERNEL):
         taps = picks(
@@ -317,9 +321,10 @@
         pooled = jnp.concatenate([pooled, jnp.zeros((own2, c2 - c1), F32)], axis=1)
     enc_ref[0] = (enc + pooled).astype(BF16)
 
-    gain_twin.wait_recv()
-    gbuf[2] = gbuf[0] + gbuf[1]
-    gain_across.start()
+    gain_across.wait_recv()
+    gbuf[4 + far] = gbuf[2] + gbuf[3]
+    for d in range(1, outer):
+        gain_far(d, 1).start()
     c_across()
 
     def taps_of(read, rows, length):
@@ -363,10 +368,6 @@
 
     lax.fori_loop(1, n, a_done, 0)
     stack1 = taps_of(lambda s: padded(arecv1[s].astype(F32), pad1), pad1, own1)
-    gain_across.wait_recv()
-    gbuf[4 + far] = gbuf[2] + gbuf[3]
-    for d in range(1, outer):
-        gain_far(d, 1).start()
     u_finish()
     lax.fori_loop(1, n, b_done, 0)
     stack2 = taps_of(unfolded, pad2, own2)

time: 46.8 us -> 39.9 us (0.85)
  Pallas kernels: 45.9 us -> 39.1 us
    pallas_call x1, Pallas kernels: 43.3 us -> 36.5 us  [shards(): pl.pallas_call(functools.partial(kernel, n), out_shape=(jax.ShapeDtypeStr...]
where the time goes in v4:
time: 39.9 us; the launch traced here: 39.8 us
  Pallas kernels  39.1 us (98%)
  between operations  0.64 us (2%)
    pallas_call x1, Pallas kernels, shards(): pl.pallas_call(functools.partial(kernel, n), out_shape=(jax.ShapeDtypeStr...  36.5 us
    pallas_call x1, Pallas kernels, shards(): pl.pallas_call(place_results, out_shape=tuple((jax.ShapeDtypeStruct(r.sha...  2.6 us

profile of v4, /device:TPU:0, one launch (start us, length us, event | category | flops | bytes accessed | tf_op | source)
XLA Modules:
  0.0 39.8 jit_solution(4230636330743031299)
XLA Ops:
  0.6 36.5 %shard_map.109 = (bf16[1,32,768]{2,1,0:T(8,128)(2,1)}, bf16[1,128,640]{2,1,0:T(8,128)(2,1)}, f32[40,3840]{1,0:T(8,128)}, f32[48,3840]{1,0:T(8,128)}, f32[640]{0:T(1024)}, /*index=5*/f32[768]{0:T(1024)}) custom-call(bf16[1,128,640]{2,1,0:T(8,128)(2,1)} %x_ref.1, f32[640]{0:T(1024)} %g1_ref.1, bf16[640,3840]{1,0:T(8,128)(2,1)} %w1_hbm.1, f32[768]{0:T(1024)} %g2_ref.1, ...), custom_call_target="tpu_custom_call" | custom-call | tf_op jit(solution)/shard_map/pallas_call | solution.py:431
  37.1 2.6 %shard_map.110 = (bf16[1,32,768]{2,1,0:T(8,128)(2,1)}, bf16[1,128,640]{2,1,0:T(8,128)(2,1)}, f32[40,3840]{1,0:T(8,128)}, f32[48,3840]{1,0:T(8,128)}, f32[640]{0:T(1024)}, /*index=5*/f32[768]{0:T(1024)}) custom-call(bf16[1,32,768]{2,1,0:T(8,128)(2,1)} %get-tuple-element.12.refs_0_, bf16[1,128,640]{2,1,0:T(8,128)(2,1)} %get-tuple-element.13.refs_1_, ...), custom_call_target="tpu_custom_call" | custom-call | tf_op jit(solution)/shard_map/pallas_call | solution.py:472
